TPU v7x, 512 devices: a whole 4x8x8 slice. The times are simulated.
512 devices in a mesh: rows: 64 (over y, x, z_hi), cols: 8 (over z_lo, core).
Axes of the slice: x: 4, y: 8, z: 8 (z_hi: 2, z_lo: 4; z = z_hi * 4 + z_lo), core: 2. Of those that a mesh axis runs over, the one named last changes fastest.
Arguments:
- cross_kernel: float32 [65536, 1024], P('rows', 'cols'), may hold values from -6 to 6
- factor_panels: float32 [2, 512, 65536], P(None, 'cols', 'rows'), may hold values from -0.25 to 0.25
- block_inverses: float32 [2, 512, 512], P(None, 'cols'), may hold values from -0.5 to 1.5, as said below
Outputs:
- solved: float32 [65536, 1024], P('rows', 'cols')
Inputs may be any that keep to these rules, and one draw needn't show every extreme that they name: `block_inverses`: each block is lower triangular, with diagonal entries from 0.5 to 1.5.
All inputs are finite; a program needn't handle non-finite values.
Results may differ from a plain program's by a relative error of at most 0.000084.
Values sent between devices are 32-bit elements; how exact they have to be, the bound alone decides.
A program may use at most 64 MiB of HBM per device.

v0:
```python
import jax
import jax.numpy as jnp
from jax import lax
from jax.sharding import PartitionSpec as P

highest = lax.Precision.HIGHEST


def spread(array, axis, root):
    mine = lax.axis_index(axis) == root
    return lax.psum(jnp.where(mine, array, jnp.zeros_like(array)), axis)


def contract_rows(left, right):
    return lax.dot_general(
        left, right, (((0,), (0,)), ((), ())), precision=highest, preferred_element_type=jnp.float32
    )


def diagonal_solve(inverse_rows, rhs_block):
    return jnp.dot(
        lax.all_gather(inverse_rows, "cols", axis=0, tiled=True),
        rhs_block,
        precision=highest,
        preferred_element_type=jnp.float32,
    )


def share_block(solved_rows):
    return spread(solved_rows, "rows", 0)


def second_update(factor_rows, solved_rows):
    return contract_rows(lax.all_gather(factor_rows, "cols", axis=0, tiled=True), solved_rows)


def on_device(cross_kernel, factor_panels, block_inverses):
    width = block_inverses.shape[2]
    is_zero = lax.axis_index("rows") == 0
    first_factor = lax.all_gather(factor_panels[0], "cols", axis=0, tiled=True)
    first = share_block(diagonal_solve(block_inverses[0], cross_kernel[:width]))
    fresh = cross_kernel - contract_rows(first_factor, first)
    current = jnp.concatenate([jnp.where(is_zero, first, fresh[:width]), fresh[width:]], axis=0)
    second = share_block(diagonal_solve(block_inverses[1], current[width : 2 * width]))
    fresh = current - second_update(factor_panels[1], second)
    top = jnp.where(is_zero, current[:width], fresh[:width])
    middle = jnp.where(is_zero, second, fresh[width : 2 * width])
    return jnp.concatenate([top, middle, fresh[2 * width :]], axis=0)


def solution(mesh):
    in_specs = (P("rows", "cols"), P(None, "cols", "rows"), P(None, "cols", None))
    out_specs = P("rows", "cols")
    return jax.shard_map(
        on_device, mesh=mesh, in_specs=in_specs, out_specs=out_specs, check_vma=False
    )
```

profile of v0, /device:TPU:16, one launch (start us, length us, event | category | flops | bytes accessed | tf_op | source)
XLA Modules:
  0.0 1783.4 jit_solution(6935677184264947465)
XLA Ops:
  6.5 0.0 copy-start
  6.5 0.0 copy-start.3
  6.5 0.0 all-gather.9.cloned.1.call-start
  6.5 1.8 fusion.22
  8.3 0.0 all-gather.9.cloned.1.call-update
  8.3 0.0 all-reduce.3.cloned.1.call-start
  8.4 45.9 %all-gather.9.cloned.1.call-done = f32[1,512,512]{2,1,0:T(8,128)} async-done(((f32[1,64,512]{2,1,0:T(8,128)}), f32[1,512,512]{2,1,0:T(8,128)}) %all-gather.9.cloned.1.call-update) | async-done | bytes 1048592 | tf_op jit(solution)/shard_map/all_gather | solution.py:22
  54.3 3.0 convolution_select_fusion.1
  57.2 0.0 all-reduce.3.cloned.1.call-update
  57.3 0.0 all-gather.11.cloned.1.call-start
  57.3 0.0 copy-done.3
  57.3 0.8 fusion.21
  58.1 0.0 all-gather.11.cloned.1.call-update
  58.2 0.0 all-gather.13.cloned.1.call-start
  58.2 0.5 all-gather.13.cloned.1.call-update
  58.7 0.0 all-gather.15.cloned.1.call-start
  58.8 0.5 all-gather.15.cloned.1.call-update
  59.3 0.0 all-reduce.5.cloned.1.call-start
  59.4 790.3 %all-reduce.3.cloned.1.call-done = f32[512,128]{1,0:T(8,128)} async-done(((f32[512,128]{1,0:T(8,128)}), f32[512,128]{1,0:T(8,128)}) %all-reduce.3.cloned.1.call-update) | async-done | bytes 262160 | tf_op jit(solution)/shard_map/psum | solution.py:11
  849.6 0.0 copy-start.1
  849.6 39.9 %all-gather.11.cloned.1.call-done = f32[1,512,1024]{2,1,0:T(8,128)} async-done(((f32[1,64,1024]{2,1,0:T(8,128)}), f32[1,512,1024]{2,1,0:T(8,128)}) %all-gather.11.cloned.1.call-update) | async-done | bytes 2097168 | tf_op jit(solution)/shard_map/all_gather | solution.py:40
  889.5 0.0 copy-done
  889.5 5.1 fusion.13
  894.6 36.7 %all-gather.13.cloned.1.call-done = f32[1,512,512]{2,1,0:T(8,128)} async-done(((f32[1,64,512]{2,1,0:T(8,128)}), f32[1,512,512]{2,1,0:T(8,128)}) %all-gather.13.cloned.1.call-update) | async-done | bytes 1048592 | tf_op jit(solution)/shard_map/all_gather | solution.py:22
  931.4 2.9 fusion.16
  934.3 0.0 all-reduce.5.cloned.1.call-update
  934.3 0.0 copy-done.1
  934.4 40.0 %all-gather.15.cloned.1.call-done = f32[1,512,1024]{2,1,0:T(8,128)} async-done(((f32[1,64,1024]{2,1,0:T(8,128)}), f32[1,512,1024]{2,1,0:T(8,128)}) %all-gather.15.cloned.1.call-update) | async-done | bytes 2097168 | tf_op jit(solution)/shard_map/all_gather | solution.py:34
  974.4 796.1 %all-reduce.5.cloned.1.call-done = f32[512,128]{1,0:T(8,128)} async-done(((f32[512,128]{1,0:T(8,128)}), f32[512,128]{1,0:T(8,128)}) %all-reduce.5.cloned.1.call-update) | async-done | bytes 262160 | tf_op jit(solution)/shard_map/psum | solution.py:11
  1770.5 0.0 copy-start.2
  1770.5 5.1 fusion.10
  1775.7 0.0 copy-done.2
  1775.7 0.1 slice_select_fusion.1
  1775.7 0.0 copy-start.4
  1775.8 0.8 copy-done.4
  (2 shorter events, 0.0 us)
Async XLA Ops:
  6.5 883.0 %copy-start = (f32[1024,128]{1,0:T(8,128)S(1)}, f32[1024,128]{1,0:T(8,128)}, u32[]{:S(2)}) copy-start(f32[1024,128]{1,0:T(8,128)} %param.3) | copy-start | bytes 1572868
  6.5 50.8 %copy-start.3 = (f32[2,64,1024]{2,1,0:T(8,128)S(1)}, f32[2,64,1024]{2,1,0:T(8,128)}, u32[]{:S(2)}) copy-start(f32[2,64,1024]{2,1,0:T(8,128)} %param.4) | copy-start | bytes 1572868
  6.5 47.7 %all-gather.9.cloned.1.call-start = ((), (), s32[]{:S(2)}) async-start(), calls=%async_computation.2 | async-start | bytes 1179648 | tf_op jit(solution)/shard_map/all_gather | solution.py:22
  8.3 841.3 %all-reduce.3.cloned.1.call-start = ((), (), s32[]{:S(2)}) async-start(), calls=%async_computation | async-start | bytes 524288 | tf_op jit(solution)/shard_map/psum | solution.py:11
  57.3 832.2 %all-gather.11.cloned.1.call-start = ((), (), s32[]{:S(2)}) async-start(), calls=%async_computation.3 | async-start | bytes 2359296 | tf_op jit(solution)/shard_map/all_gather | solution.py:40
  58.2 873.2 %all-gather.13.cloned.1.call-start = ((), (), s32[]{:S(2)}) async-start(), calls=%async_computation.4 | async-start | bytes 1179648 | tf_op jit(solution)/shard_map/all_gather | solution.py:22
  58.7 915.7 %all-gather.15.cloned.1.call-start = ((), (), s32[]{:S(2)}) async-start(), calls=%async_computation.5 | async-start | bytes 2359296 | tf_op jit(solution)/shard_map/all_gather | solution.py:34
  59.3 1711.2 %all-reduce.5.cloned.1.call-start = ((), (), s32[]{:S(2)}) async-start(), calls=%async_computation.1 | async-start | bytes 524288 | tf_op jit(solution)/shard_map/psum | solution.py:11
  849.6 84.7 %copy-start.1 = (f32[512,128]{1,0:T(8,128)S(1)}, f32[512,128]{1,0:T(8,128)}, u32[]{:S(2)}) copy-start(f32[512,128]{1,0:T(8,128)} %all-reduce.3.cloned.1.call-done) | copy-start | bytes 786436
  1770.5 5.2 copy-start.2
  1775.7 0.8 copy-start.4
Sparse Core Ops, SparseCore 0:
  9.4 44.7 all-gather.8
  57.4 792.2 all-reduce.2
  851.9 37.5 all-gather.10
  891.6 39.6 all-gather.12
  933.5 40.8 all-gather.14
  977.4 793.0 all-reduce.4
where the time goes:
time: 1780 us
  waiting for transfers between devices  1750 us (98%)
    psum x2, waiting for transfers between devices, spread(): return lax.psum(jnp.where(mine, array, jnp.zeros_like(array)), axis)  1590 us
    all_gather x2, waiting for transfers between devices, diagonal_solve(): lax.all_gather(inverse_rows, 'cols', axis=0, tiled=True)  82.6 us
    all_gather x1, waiting for transfers between devices, second_update(): lax.all_gather(factor_rows, 'cols', axis=0, tiled=True)  40 us
    all_gather x1, waiting for transfers between devices, on_device(): first_factor = lax.all_gather(factor_panels[0], 'cols', axis=0, tiled=True)  39.9 us
  transfers between devices with their start and end apart: 6, of which 6 were waited for; matrix products, arithmetic and copies ran while one was open for 0% of the time, Pallas kernels for 0%

commit v1 on v0

--- a/solution.py
+++ b/solution.py
@@ -6,9 +6,15 @@
 highest = lax.Precision.HIGHEST
 
 
+def gather_and_add(shard, name):
+    parts = lax.all_gather(shard, name, axis=0, tiled=False)
+    total = parts.sum(axis=0)
+    return total
+
+
 def spread(array, axis, root):
     mine = lax.axis_index(axis) == root
-    return lax.psum(jnp.where(mine, array, jnp.zeros_like(array)), axis)
+    return gather_and_add(jnp.where(mine, array, jnp.zeros_like(array)), axis)
 
 
 def contract_rows(left, right):

time: 1780 us -> 802 us (0.45)
  the two profiles are of different devices: /device:TPU:16 before, /device:TPU:2 now
where the time goes in v1:
time: 802 us; the launch traced here: 801 us
  waiting for transfers between devices  735 us (92%)
  local copies, waits for them, and re-layouts  21.2 us (3%)
  matrix products  16.2 us (2%)
  other arithmetic  15.5 us (2%)
  between operations  13.5 us (2%)
    all_gather x2, waiting for transfers between devices, gather_and_add(): parts = lax.all_gather(shard, name, axis=0, tiled=False)  608 us
    all_gather x2, waiting for transfers between devices, diagonal_solve(): lax.all_gather(inverse_rows, 'cols', axis=0, tiled=True)  82.7 us
    all_gather x1, waiting for transfers between devices, on_device(): first_factor = lax.all_gather(factor_panels[0], 'cols', axis=0, tiled=True)  31.9 us
    unnamed x7, local copies, waits for them, and re-layouts  18.5 us
  transfers between devices with their start and end apart: 6, of which 6 were waited for; matrix products, arithmetic and copies ran while one was open for 5% of the time, Pallas kernels for 0%

profile of v1, /device:TPU:2, one launch (start us, length us, event | category | flops | bytes accessed | tf_op | source)
XLA Modules:
  0.0 801.5 jit_solution(8733493169785914782)
XLA Ops:
  6.5 0.0 copy-start.1
  6.5 0.0 all-gather.13.cloned.1.call-start
  6.5 1.7 fusion.22
  8.3 0.0 all-gather.13.cloned.1.call-update
  8.3 0.0 all-gather.15.cloned.1.call-start
  8.4 46.1 %all-gather.13.cloned.1.call-done = f32[1,512,512]{2,1,0:T(8,128)} async-done(((f32[1,64,512]{2,1,0:T(8,128)}), f32[1,512,512]{2,1,0:T(8,128)}) %all-gather.13.cloned.1.call-update) | async-done | bytes 1048592 | tf_op jit(solution)/shard_map/all_gather | solution.py:28
  54.4 3.0 convolution_select_fusion.1
  57.4 0.0 all-gather.15.cloned.1.call-update
  57.4 0.0 all-gather.17.cloned.1.call-start
  57.5 0.0 copy-done.1
  57.5 0.9 fusion.21
  58.3 0.0 all-gather.17.cloned.1.call-update
  58.4 0.0 all-gather.19.cloned.1.call-start
  58.4 0.5 all-gather.19.cloned.1.call-update
  58.9 0.0 all-gather.21.cloned.1.call-start
  59.0 298.0 %all-gather.15.cloned.1.call-done = f32[32768,128]{1,0:T(8,128)} async-done(((f32[512,128]{1,0:T(8,128)}), f32[32768,128]{1,0:T(8,128)}) %all-gather.15.cloned.1.call-update) | async-done | bytes 16777232 | tf_op jit(solution)/shard_map/all_gather | solution.py:10
  357.0 0.0 copy-start
  357.0 6.6 reduce_sum.18
  363.6 31.9 %all-gather.17.cloned.1.call-done = f32[1,512,1024]{2,1,0:T(8,128)} async-done(((f32[1,64,1024]{2,1,0:T(8,128)}), f32[1,512,1024]{2,1,0:T(8,128)}) %all-gather.17.cloned.1.call-update) | async-done | bytes 2097168 | tf_op jit(solution)/shard_map/all_gather | solution.py:46
  395.4 0.0 copy-done
  395.4 5.0 fusion.13
  400.5 36.6 %all-gather.19.cloned.1.call-done = f32[1,512,512]{2,1,0:T(8,128)} async-done(((f32[1,64,512]{2,1,0:T(8,128)}), f32[1,512,512]{2,1,0:T(8,128)}) %all-gather.19.cloned.1.call-update) | async-done | bytes 1048592 | tf_op jit(solution)/shard_map/all_gather | solution.py:28
  437.1 3.2 fusion.16
  440.3 0.0 all-gather.21.cloned.1.call-update
  440.3 0.2 all-gather.23.cloned.1.call-start
  440.5 0.3 all-gather.23.cloned.1.call-update
  440.9 309.7 %all-gather.21.cloned.1.call-done = f32[32768,128]{0,1:T(8,128)} async-done(((f32[512,128]{0,1:T(8,128)}), f32[32768,128]{0,1:T(8,128)}) %all-gather.21.cloned.1.call-update) | async-done | bytes 16777232 | tf_op jit(solution)/shard_map/all_gather | solution.py:10
  750.6 17.7 %copy.11 = f32[16,8,64,512]{3,2,1,0:T(8,128)} copy(f32[16,8,64,512]{3,1,2,0:T(8,128)} %bitcast.39) | data formatting | bytes 33554432
  768.3 8.8 %bitcast_reduce_fusion = f32[512,128]{0,1:T(8,128)S(1)} fusion(f32[16,8,64,512]{3,2,1,0:T(8,128)} %copy.11), kind=kLoop, calls=%fused_computation | loop fusion | flops 4128768 | bytes 17039360 | tf_op jit(solution)/shard_map/reduce_sum | solution.py:11
  777.1 0.1 copy.8
  777.2 11.5 %all-gather.23.cloned.1.call-done = f32[1,512,1024]{2,1,0:T(8,128)} async-done(((f32[1,64,1024]{2,1,0:T(8,128)}), f32[1,512,1024]{2,1,0:T(8,128)}) %all-gather.23.cloned.1.call-update) | async-done | bytes 2097168 | tf_op jit(solution)/shard_map/all_gather | solution.py:40
  788.7 5.0 fusion.10
  793.7 0.1 slice_select_fusion.1
  793.8 0.0 copy-start.2
  793.8 0.8 copy-done.2
  (2 shorter events, 0.0 us)
Async XLA Ops:
  6.5 50.9 %copy-start.1 = (f32[2,64,1024]{2,1,0:T(8,128)S(1)}, f32[2,64,1024]{2,1,0:T(8,128)}, u32[]{:S(2)}) copy-start(f32[2,64,1024]{2,1,0:T(8,128)} %param.4) | copy-start | bytes 1572868
  6.5 47.9 %all-gather.13.cloned.1.call-start = ((), (), s32[]{:S(2)}) async-start(), calls=%async_computation | async-start | bytes 1179648 | tf_op jit(solution)/shard_map/all_gather | solution.py:28
  8.3 348.7 %all-gather.15.cloned.1.call-start = ((), (), s32[]{:S(2)}) async-start(), calls=%async_computation.1 | async-start | bytes 17039360 | tf_op jit(solution)/shard_map/all_gather | solution.py:10
  57.4 338.0 %all-gather.17.cloned.1.call-start = ((), (), s32[]{:S(2)}) async-start(), calls=%async_computation.2 | async-start | bytes 2359296 | tf_op jit(solution)/shard_map/all_gather | solution.py:46
  58.4 378.7 %all-gather.19.cloned.1.call-start = ((), (), s32[]{:S(2)}) async-start(), calls=%async_computation.3 | async-start | bytes 1179648 | tf_op jit(solution)/shard_map/all_gather | solution.py:28
  58.9 691.7 %all-gather.21.cloned.1.call-start = ((), (), s32[]{:S(2)}) async-start(), calls=%async_computation.4 | async-start | bytes 17039360 | tf_op jit(solution)/shard_map/all_gather | solution.py:10
  357.0 38.5 %copy-start = (f32[1024,128]{1,0:T(8,128)S(1)}, f32[1024,128]{1,0:T(8,128)}, u32[]{:S(2)}) copy-start(f32[1024,128]{1,0:T(8,128)} %param.3) | copy-start | bytes 1572868
  440.3 348.4 %all-gather.23.cloned.1.call-start = ((), (), s32[]{:S(2)}) async-start(), calls=%async_computation.5 | async-start | bytes 2359296 | tf_op jit(solution)/shard_map/all_gather | solution.py:40
  793.8 0.8 copy-start.2
Sparse Core Ops, SparseCore 0:
  9.4 44.9 all-gather.12
  59.0 297.9 all-gather.14
  359.1 36.3 all-gather.16
  397.4 39.6 all-gather.18
  441.3 309.2 all-gather.20
  752.5 36.1 all-gather.22
